TPU v7x, 32 devices: a whole 2x2x4 slice. The times are simulated.
32 devices in a mesh: row: 8 (over y, x, core), col: 4 (over z).
Axes of the slice: x: 2, y: 2, z: 4, core: 2. Of those that a mesh axis runs over, the one named last changes fastest.
Arguments:
- built: bfloat16 [4096, 4096], P('row', 'col'), may hold values from -0.59765625 to 0.59765625
- build_order: int32 [32], replicated, may hold values from 0 to 31, each once
- p_pattern: int32 [32, 32], replicated, may hold values from 0 to 1, as said below
- q_pattern: int32 [32, 32], replicated, may hold values from 0 to 1, as said below
Outputs:
- purified: bfloat16 [4096, 4096], P('row', 'col')
Inputs may be any that keep to these rules, and one draw needn't show every extreme that they name: p_pattern is symmetric and 1 on the diagonal; p_pattern[i, j] is 0 unless the distance of i and j counted round the 32 blocks, or that of i and j + 16, is at most 1. q_pattern[i, j] is 0 unless the distance of i and j counted round the 32 blocks, or that of i and j + 16, is at most 2.
All inputs are finite; a program needn't handle non-finite values.
Results may differ from a plain program's by a relative error of at most 0.0045.
Values may be sent and summed in bfloat16 or wider, within the bound.
A program may use at most 128 MiB of HBM per device.

v0:
```python
import jax
import jax.numpy as jnp
from jax import lax
from jax.sharding import PartitionSpec as P

BS = 128


def contract(col_panel, portion):
    return jnp.dot(portion, col_panel, preferred_element_type=jnp.float32)


def body(built, build_order, p_pattern, q_pattern):
    row_count = built.shape[0] // BS
    col_count = built.shape[1] // BS
    block_count = build_order.shape[0]
    row_index = lax.axis_index("row")
    col_index = lax.axis_index("col")
    build_slab = lax.all_gather(built, "row", axis=0, tiled=True)
    blocks = build_slab.reshape(block_count, BS, col_count * BS)
    inverse = (
        jnp.zeros((block_count,), jnp.int32)
        .at[build_order]
        .set(jnp.arange(block_count, dtype=jnp.int32))
    )
    col_mask = lax.dynamic_slice_in_dim(p_pattern, col_index * col_count, col_count, 1).astype(
        jnp.bfloat16
    )
    ordered = blocks[inverse].reshape(block_count, BS, col_count, BS)
    columns = (ordered * col_mask[:, None, :, None]).reshape(block_count * BS, col_count * BS)
    start_block = row_index * row_count
    local_tile = lax.dynamic_slice_in_dim(columns, start_block * BS, row_count * BS, 0)
    q_block = lax.dynamic_slice(
        q_pattern, (start_block, col_index * col_count), (row_count, col_count)
    ).astype(jnp.float32)
    q_tile = jnp.broadcast_to(q_block[:, None, :, None], (row_count, BS, col_count, BS)).reshape(
        row_count * BS, col_count * BS
    )
    square = contract(columns, lax.all_gather(local_tile, "col", axis=1, tiled=True)) * q_tile
    rounded = square.astype(jnp.bfloat16)
    cubed_term = contract(columns, lax.all_gather(rounded, "col", axis=1, tiled=True))
    return ((3.0 * square - 2.0 * cubed_term) * q_tile).astype(jnp.bfloat16)


def solution(mesh):
    placed = (P("row", "col"), P(), P(), P())
    return jax.shard_map(
        body, mesh=mesh, in_specs=placed, out_specs=P("row", "col"), check_vma=False
    )
```

profile of v0, /device:TPU:0, one launch (start us, length us, event | category | flops | bytes accessed | tf_op | source)
XLA Modules:
  0.0 273.1 jit_solution(3212071331895305885)
XLA Ops:
  6.5 0.0 all-gather.4.cloned.1.call-start
  6.5 0.7 all-gather.4.cloned.1.call-update
  7.3 0.0 all-gather.6.cloned.1.call-start
  7.3 0.7 compare_select_fusion.1
  8.0 0.7 scatter_custom_fusion
  8.7 0.8 dynamic-slice_convert_fusion
  9.5 56.8 %all-gather.4.cloned.1.call-done = bf16[4096,1024]{1,0:T(8,128)(2,1)} async-done(((bf16[512,1024]{1,0:T(8,128)(2,1)}), bf16[4096,1024]{1,0:T(8,128)(2,1)}) %all-gather.4.cloned.1.call-update) | async-done | bytes 8388624 | tf_op jit(solution)/shard_map/all_gather | solution.py:19
  66.2 8.4 %gather_fusion = bf16[32,128,1024]{2,1,0:T(8,128)(2,1)} fusion(bf16[32,128,1024]{2,1,0:T(8,128)(2,1)} %bitcast.23, s32[1024]{0:T(1024)S(1)} %pad_clamp_fusion), kind=kCustom, calls=%fused_computation | custom fusion | bytes 16777344 | tf_op jit(solution)/shard_map/gather | solution.py:29
  74.6 0.0 copy-start
  74.7 1.1 mul.40
  75.8 2.2 copy-done
  78.0 1.9 bitcast_multiply_fusion
  79.9 0.0 copy-start.1
  80.0 3.2 %copy-done.1 = bf16[4096,1024]{1,0:T(8,128)(2,1)} copy-done((bf16[4096,1024]{1,0:T(8,128)(2,1)}, bf16[4096,1024]{1,0:T(8,128)(2,1)S(1)}, u32[]{:S(2)}) %copy-start.1) | copy-done | bytes 8388632
  83.2 1.0 constant_dynamic-slice_fusion
  84.2 0.0 all-gather.6.cloned.1.call-update
  84.2 0.0 all-gather.8.cloned.1.call-start
  84.3 0.8 dynamic-slice_convert_fusion.1
  85.1 80.1 %all-gather.6.cloned.1.call-done = bf16[512,4096]{1,0:T(8,128)(2,1)} async-done(((bf16[512,1024]{1,0:T(8,128)(2,1)}), bf16[512,4096]{1,0:T(8,128)(2,1)}) %all-gather.6.cloned.1.call-update) | async-done | bytes 4194320 | tf_op jit(solution)/shard_map/all_gather | solution.py:39
  165.1 0.2 broadcast_in_dim.15
  165.3 10.9 %fusion.1 = (bf16[512,1024]{1,0:T(8,128)(2,1)}, f32[512,1024]{1,0:T(8,128)}) fusion(f32[64,8,8,128]{3,2,1,0:T(8,128)S(1)} %bitcast.24, bf16[512,4096]{1,0:T(8,128)(2,1)} %all-gather.6.cloned.1.call-done, bf16[4096,1024]{1,0:T(8,128)(2,1)} %copy-done.1), kind=kOutput, calls=%fused_computation.6 | convolution fusion | flops 4296015872 | bytes 17825792 | tf_op jit(solution)/shard_map/dot_general | solution.py:10
  176.3 0.0 all-gather.8.cloned.1.call-update
  176.3 79.4 %all-gather.8.cloned.1.call-done = bf16[512,4096]{1,0:T(8,128)(2,1)} async-done(((bf16[512,1024]{1,0:T(8,128)(2,1)}), bf16[512,4096]{1,0:T(8,128)(2,1)}) %all-gather.8.cloned.1.call-update) | async-done | bytes 4194320 | tf_op jit(solution)/shard_map/all_gather | solution.py:41
  255.7 10.9 %fusion = bf16[512,1024]{1,0:T(8,128)(2,1)} fusion(f32[64,8,8,128]{3,2,1,0:T(8,128)S(1)} %bitcast.25, f32[512,1024]{1,0:T(8,128)} %get-tuple-element.6, bf16[512,4096]{1,0:T(8,128)(2,1)} %all-gather.8.cloned.1.call-done, bf16[4096,1024]{1,0:T(8,128)(2,1)} %copy-done.1), kind=kOutput, calls=%fused_computation.5 | convolution fusion | flops 4298113024 | bytes 17825792 | tf_op jit(solution)/shard_map/dot_general | solution.py:10
  (3 shorter events, 0.0 us)
Async XLA Ops:
  6.5 59.7 %all-gather.4.cloned.1.call-start = ((), (), s32[]{:S(2)}) async-start(), calls=%async_computation | async-start | bytes 9437184 | tf_op jit(solution)/shard_map/all_gather | solution.py:19
  7.3 157.9 %all-gather.6.cloned.1.call-start = ((), (), s32[]{:S(2)}) async-start(), calls=%async_computation.1 | async-start | bytes 5242880 | tf_op jit(solution)/shard_map/all_gather | solution.py:39
  74.6 3.4 %copy-start = (bf16[32,128,1024]{2,1,0:T(8,128)(2,1)S(1)}, bf16[32,128,1024]{2,1,0:T(8,128)(2,1)}, u32[]{:S(2)}) copy-start(bf16[32,128,1024]{2,1,0:T(8,128)(2,1)} %gather_fusion) | copy-start | bytes 25165828
  79.9 3.2 %copy-start.1 = (bf16[4096,1024]{1,0:T(8,128)(2,1)}, bf16[4096,1024]{1,0:T(8,128)(2,1)S(1)}, u32[]{:S(2)}) copy-start(bf16[4096,1024]{1,0:T(8,128)(2,1)S(1)} %bitcast_multiply_fusion) | copy-start | bytes 25165828
  84.2 171.4 %all-gather.8.cloned.1.call-start = ((), (), s32[]{:S(2)}) async-start(), calls=%async_computation.2 | async-start | bytes 5242880 | tf_op jit(solution)/shard_map/all_gather | solution.py:41
Sparse Core Ops, SparseCore 0:
  9.2 56.9 all-gather.3
  84.4 80.7 all-gather.5
  176.4 79.2 all-gather.7
where the time goes:
time: 273 us
  waiting for transfers between devices  217 us (79%)
  matrix products  21.8 us (8%)
  local copies, waits for them, and re-layouts  16.9 us (6%)
  between operations  13.2 us (5%)
  other arithmetic  4.14 us (2%)
    all_gather x1, waiting for transfers between devices, body(): lax.all_gather(local_tile, 'col', axis=1, tiled=True)  80.1 us
    all_gather x1, waiting for transfers between devices, body(): lax.all_gather(rounded, 'col', axis=1, tiled=True)  79.4 us
    all_gather x1, waiting for transfers between devices, body(): build_slab = lax.all_gather(built, 'row', axis=0, tiled=True)  56.8 us
    dot_general x2, matrix products, contract(): return jnp.dot(portion, col_panel, preferred_element_type=jnp.float32)  21.8 us
    gather x1, local copies, waits for them, and re-layouts, body(): ordered = blocks[inverse].reshape(block_count, BS, col_count, BS)  8.42 us
  transfers between devices with their start and end apart: 3, of which 3 were waited for; matrix products, arithmetic and copies ran while one was open for 1% of the time, Pallas kernels for 0%

commit v1 on v0

--- a/solution.py
+++ b/solution.py
@@ -4,6 +4,12 @@
 from jax.sharding import PartitionSpec as P
 
 BS = 128
+
+
+def gather_from_all(x, axis, dim):
+    size = lax.axis_size(axis)
+    repeats = [size if d == dim else 1 for d in range(x.ndim)]
+    return lax.all_to_all(jnp.tile(x, repeats), axis, split_axis=dim, concat_axis=dim, tiled=True)
 
 
 def contract(col_panel, portion):
@@ -16,7 +22,7 @@
     block_count = build_order.shape[0]
     row_index = lax.axis_index("row")
     col_index = lax.axis_index("col")
-    build_slab = lax.all_gather(built, "row", axis=0, tiled=True)
+    build_slab = gather_from_all(built, "row", 0)
     blocks = build_slab.reshape(block_count, BS, col_count * BS)
     inverse = (
         jnp.zeros((block_count,), jnp.int32)

time: 273 us -> 320 us (1.17)
  waiting for transfers between devices: 217 us -> 253 us
  local copies, waits for them, and re-layouts: 16.9 us -> 22.5 us
  starting transfers between devices: 0.08 us -> 5.41 us
    all_to_all x0 -> x1, waiting for transfers between devices: none -> 93.7 us  [gather_from_all(): lax.all_to_all(jnp.tile(x, repeats), axis, split_axis=dim, concat_axis=di...]
    all_gather x1 -> x0, waiting for transfers between devices: 56.8 us -> none  [body(): build_slab = lax.all_gather(built, 'row', axis=0, tiled=True)]
    another operation x0 -> x1, local copies, waits for them, and re-layouts: none -> 5.55 us  [gather_from_all(): jnp.tile(x, repeats)]
    all_to_all x0 -> x1, starting transfers between devices: none -> 5.33 us  [gather_from_all(): lax.all_to_all(jnp.tile(x, repeats), axis, split_axis=dim, concat_axis=di...]
  transfers between devices with their start and end apart: 3 -> 3, of which waited for: 3 -> 3; matrix products, arithmetic and copies ran while one was open for 1% -> 0% of each run, Pallas kernels for 0% -> 0%
where the time goes in v1:
time: 320 us; the launch traced here: 319 us
  waiting for transfers between devices  253 us (79%)
  local copies, waits for them, and re-layouts  22.5 us (7%)
  matrix products  21.8 us (7%)
  between operations  13.5 us (4%)
  starting transfers between devices  5.41 us (2%)
    all_to_all x1, waiting for transfers between devices, gather_from_all(): lax.all_to_all(jnp.tile(x, repeats), axis, split_axis=dim, concat_axis=di...  93.7 us
    all_gather x1, waiting for transfers between devices, body(): lax.all_gather(local_tile, 'col', axis=1, tiled=True)  80.2 us
    all_gather x1, waiting for transfers between devices, body(): lax.all_gather(rounded, 'col', axis=1, tiled=True)  79.4 us
    dot_general x2, matrix products, contract(): return jnp.dot(portion, col_panel, preferred_element_type=jnp.float32)  21.8 us
    gather x1, local copies, waits for them, and re-layouts, body(): ordered = blocks[inverse].reshape(block_count, BS, col_count, BS)  8.41 us
  transfers between devices with their start and end apart: 3, of which 3 were waited for; matrix products, arithmetic and copies ran while one was open for 0% of the time, Pallas kernels for 0%

profile of v1, /device:TPU:0, one launch (start us, length us, event | category | flops | bytes accessed | tf_op | source)
XLA Modules:
  0.0 319.3 jit_solution(10148122835149871096)
XLA Ops:
  6.5 5.5 %tile.2 = bf16[8,512,1024]{2,1,0:T(8,128)(2,1)} broadcast(bf16[512,1024]{1,0:T(8,128)(2,1)} %param.4), dimensions={1,2} | broadcast | bytes 9437184 | tf_op jit(solution)/shard_map/tile | solution.py:12
  12.1 0.0 copy-start.3
  12.1 0.0 copy-start.2
  12.1 5.3 %all-to-all-start = ((bf16[8,512,1024]{2,1,0:T(8,128)(2,1)}), bf16[8,512,1024]{2,1,0:T(8,128)(2,1)}, u32[]{:S(2)}, u32[]{:S(2)}) async-start(bf16[8,512,1024]{2,1,0:T(8,128)(2,1)} %tile.2), calls=%async_computation | async-start | bytes 16777216 | tf_op jit(solution)/shard_map/all_to_all | solution.py:12
  17.4 0.0 all-gather.3.cloned.1.call-start
  17.5 0.0 copy-done.3
  17.5 0.7 scatter_custom_fusion
  18.2 0.0 copy-done.2
  18.2 0.1 dynamic-slice_convert_fusion
  18.3 93.7 %all-to-all-done = bf16[8,512,1024]{2,1,0:T(8,128)(2,1)} async-done(((bf16[8,512,1024]{2,1,0:T(8,128)(2,1)}), bf16[8,512,1024]{2,1,0:T(8,128)(2,1)}, u32[]{:S(2)}, u32[]{:S(2)}) %all-to-all-start) | async-done | bytes 8388640 | tf_op jit(solution)/shard_map/all_to_all | solution.py:12
  112.0 8.4 %gather_fusion = bf16[32,128,1024]{2,1,0:T(8,128)(2,1)} fusion(bf16[32,128,1024]{2,1,0:T(8,128)(2,1)} %bitcast, s32[1024]{0:T(1024)S(1)} %pad_clamp_fusion), kind=kCustom, calls=%fused_computation | custom fusion | bytes 16777344 | tf_op jit(solution)/shard_map/gather | solution.py:35
  120.4 0.0 copy-start
  120.4 1.1 mul.40
  121.5 2.2 copy-done
  123.8 1.9 bitcast_multiply_fusion
  125.7 0.0 copy-start.1
  125.7 3.2 %copy-done.1 = bf16[4096,1024]{1,0:T(8,128)(2,1)} copy-done((bf16[4096,1024]{1,0:T(8,128)(2,1)}, bf16[4096,1024]{1,0:T(8,128)(2,1)S(1)}, u32[]{:S(2)}) %copy-start.1) | copy-done | bytes 8388632
  128.9 1.0 constant_dynamic-slice_fusion
  129.9 0.0 all-gather.3.cloned.1.call-update
  129.9 0.0 all-gather.5.cloned.1.call-start
  130.0 0.8 dynamic-slice_convert_fusion.1
  130.8 80.2 %all-gather.3.cloned.1.call-done = bf16[512,4096]{1,0:T(8,128)(2,1)} async-done(((bf16[512,1024]{1,0:T(8,128)(2,1)}), bf16[512,4096]{1,0:T(8,128)(2,1)}) %all-gather.3.cloned.1.call-update) | async-done | bytes 4194320 | tf_op jit(solution)/shard_map/all_gather | solution.py:45
  211.0 0.2 broadcast_in_dim.15
  211.2 10.9 %fusion.1 = (bf16[512,1024]{1,0:T(8,128)(2,1)}, f32[512,1024]{1,0:T(8,128)}) fusion(f32[64,8,8,128]{3,2,1,0:T(8,128)S(1)} %bitcast.23, bf16[512,4096]{1,0:T(8,128)(2,1)} %all-gather.3.cloned.1.call-done, bf16[4096,1024]{1,0:T(8,128)(2,1)} %copy-done.1), kind=kOutput, calls=%fused_computation.6 | convolution fusion | flops 4296015872 | bytes 17825792 | tf_op jit(solution)/shard_map/dot_general | solution.py:16
  222.1 0.0 all-gather.5.cloned.1.call-update
  222.1 79.4 %all-gather.5.cloned.1.call-done = bf16[512,4096]{1,0:T(8,128)(2,1)} async-done(((bf16[512,1024]{1,0:T(8,128)(2,1)}), bf16[512,4096]{1,0:T(8,128)(2,1)}) %all-gather.5.cloned.1.call-update) | async-done | bytes 4194320 | tf_op jit(solution)/shard_map/all_gather | solution.py:47
  301.5 10.9 %fusion = bf16[512,1024]{1,0:T(8,128)(2,1)} fusion(f32[64,8,8,128]{3,2,1,0:T(8,128)S(1)} %bitcast.24, f32[512,1024]{1,0:T(8,128)} %get-tuple-element.6, bf16[512,4096]{1,0:T(8,128)(2,1)} %all-gather.5.cloned.1.call-done, bf16[4096,1024]{1,0:T(8,128)(2,1)} %copy-done.1), kind=kOutput, calls=%fused_computation.5 | convolution fusion | flops 4298113024 | bytes 17825792 | tf_op jit(solution)/shard_map/dot_general | solution.py:16
  (4 shorter events, 0.0 us)
Async XLA Ops:
  12.1 5.4 %copy-start.3 = (s32[32]{0:T(128)S(1)}, s32[32]{0:T(128)}, u32[]{:S(2)}) copy-start(s32[32]{0:T(128)} %param.5) | copy-start | bytes 388
  12.1 6.1 %copy-start.2 = (s32[32,32]{1,0:T(8,128)S(1)}, s32[32,32]{1,0:T(8,128)}, u32[]{:S(2)}) copy-start(s32[32,32]{1,0:T(8,128)} %param.6) | copy-start | bytes 12292
  12.1 99.9 %all-to-all-start = ((bf16[8,512,1024]{2,1,0:T(8,128)(2,1)}), bf16[8,512,1024]{2,1,0:T(8,128)(2,1)}, u32[]{:S(2)}, u32[]{:S(2)}) async-start(bf16[8,512,1024]{2,1,0:T(8,128)(2,1)} %tile.2), calls=%async_computation | async-start | bytes 16777216 | tf_op jit(solution)/shard_map/all_to_all | solution.py:12
  17.4 193.5 %all-gather.3.cloned.1.call-start = ((), (), s32[]{:S(2)}) async-start(), calls=%async_computation.1 | async-start | bytes 5242880 | tf_op jit(solution)/shard_map/all_gather | solution.py:45
  120.4 3.4 %copy-start = (bf16[32,128,1024]{2,1,0:T(8,128)(2,1)S(1)}, bf16[32,128,1024]{2,1,0:T(8,128)(2,1)}, u32[]{:S(2)}) copy-start(bf16[32,128,1024]{2,1,0:T(8,128)(2,1)} %gather_fusion) | copy-start | bytes 25165828
  125.7 3.2 %copy-start.1 = (bf16[4096,1024]{1,0:T(8,128)(2,1)}, bf16[4096,1024]{1,0:T(8,128)(2,1)S(1)}, u32[]{:S(2)}) copy-start(bf16[4096,1024]{1,0:T(8,128)(2,1)S(1)} %bitcast_multiply_fusion) | copy-start | bytes 25165828
  129.9 171.6 %all-gather.5.cloned.1.call-start = ((), (), s32[]{:S(2)}) async-start(), calls=%async_computation.2 | async-start | bytes 5242880 | tf_op jit(solution)/shard_map/all_gather | solution.py:47
Sparse Core Ops, SparseCore 0:
  130.1 80.8 all-gather.2
  222.3 79.2 all-gather.4

commit v2 on v0

--- a/solution.py
+++ b/solution.py
@@ -4,6 +4,18 @@
 from jax.sharding import PartitionSpec as P
 
 BS = 128
+
+
+def collect(x, axis, dim):
+    ways, here = (lax.axis_size(axis), lax.axis_index(axis))
+    grown, reach = (x, 1)
+    while reach < ways:
+        theirs = lax.ppermute(grown, axis, [(d, d ^ reach) for d in range(ways)])
+        mine_first = jnp.concatenate([grown, theirs], axis=dim)
+        theirs_first = jnp.concatenate([theirs, grown], axis=dim)
+        grown = jnp.where(here & reach == 0, mine_first, theirs_first)
+        reach = 2 * reach
+    return grown
 
 
 def contract(col_panel, portion):
@@ -36,7 +48,7 @@
     q_tile = jnp.broadcast_to(q_block[:, None, :, None], (row_count, BS, col_count, BS)).reshape(
         row_count * BS, col_count * BS
     )
-    square = contract(columns, lax.all_gather(local_tile, "col", axis=1, tiled=True)) * q_tile
+    square = contract(columns, collect(local_tile, "col", 1)) * q_tile
     rounded = square.astype(jnp.bfloat16)
     cubed_term = contract(columns, lax.all_gather(rounded, "col", axis=1, tiled=True))
     return ((3.0 * square - 2.0 * cubed_term) * q_tile).astype(jnp.bfloat16)

time: 273 us -> 315 us (1.15)
  waiting for transfers between devices: 217 us -> 252 us
  starting transfers between devices: 0.08 us -> 4.06 us
    ppermute x0 -> x2, waiting for transfers between devices: none -> 114 us  [collect(): theirs = lax.ppermute(grown, axis, [(d, d ^ reach) for d in range(ways)])]
    all_gather x1 -> x0, waiting for transfers between devices: 80.1 us -> none  [body(): lax.all_gather(local_tile, 'col', axis=1, tiled=True)]
    ppermute x0 -> x2, starting transfers between devices: none -> 4.02 us  [collect(): theirs = lax.ppermute(grown, axis, [(d, d ^ reach) for d in range(ways)])]
  transfers between devices with their start and end apart: 3 -> 4, of which waited for: 3 -> 4; matrix products, arithmetic and copies ran while one was open for 1% -> 1% of each run, Pallas kernels for 0% -> 0%
where the time goes in v2:
time: 315 us
  waiting for transfers between devices  252 us (80%)
  matrix products  23 us (7%)
  local copies, waits for them, and re-layouts  16 us (5%)
  between operations  13.5 us (4%)
  other arithmetic  6.53 us (2%)
  starting transfers between devices  4.06 us (1%)
    ppermute x2, waiting for transfers between devices, collect(): theirs = lax.ppermute(grown, axis, [(d, d ^ reach) for d in range(ways)])  114 us
    all_gather x1, waiting for transfers between devices, body(): lax.all_gather(rounded, 'col', axis=1, tiled=True)  80.9 us
    all_gather x1, waiting for transfers between devices, body(): build_slab = lax.all_gather(built, 'row', axis=0, tiled=True)  56.8 us
    dot_general x2, matrix products, contract(): return jnp.dot(portion, col_panel, preferred_element_type=jnp.float32)  23 us
    gather x1, local copies, waits for them, and re-layouts, body(): ordered = blocks[inverse].reshape(block_count, BS, col_count, BS)  8.42 us
  transfers between devices with their start and end apart: 4, of which 4 were waited for; matrix products, arithmetic and copies ran while one was open for 1% of the time, Pallas kernels for 0%

profile of v2, /device:TPU:0, one launch (start us, length us, event | category | flops | bytes accessed | tf_op | source)
XLA Modules:
  0.0 315.1 jit_solution(16737250623659351148)
XLA Ops:
  6.5 0.0 all-gather.3.cloned.1.call-start
  6.5 0.7 all-gather.3.cloned.1.call-update
  7.3 0.0 all-gather.5.cloned.1.call-start
  7.3 0.7 compare_select_fusion.1
  8.0 0.7 scatter_custom_fusion
  8.7 0.8 dynamic-slice_convert_fusion
  9.5 56.8 %all-gather.3.cloned.1.call-done = bf16[4096,1024]{1,0:T(8,128)(2,1)} async-done(((bf16[512,1024]{1,0:T(8,128)(2,1)}), bf16[4096,1024]{1,0:T(8,128)(2,1)}) %all-gather.3.cloned.1.call-update) | async-done | bytes 8388624 | tf_op jit(solution)/shard_map/all_gather | solution.py:31
  66.2 8.4 %gather_fusion = bf16[32,128,1024]{2,1,0:T(8,128)(2,1)} fusion(bf16[32,128,1024]{2,1,0:T(8,128)(2,1)} %bitcast.22, s32[1024]{0:T(1024)S(1)} %pad_clamp_fusion), kind=kCustom, calls=%fused_computation | custom fusion | bytes 16777344 | tf_op jit(solution)/shard_map/gather | solution.py:41
  74.6 0.0 copy-start
  74.7 1.1 mul.40
  75.8 2.2 copy-done
  78.0 1.9 bitcast_multiply_fusion
  79.9 0.0 copy-start.1
  80.0 3.2 %copy-done.1 = bf16[4096,1024]{1,0:T(8,128)(2,1)} copy-done((bf16[4096,1024]{1,0:T(8,128)(2,1)}, bf16[4096,1024]{1,0:T(8,128)(2,1)S(1)}, u32[]{:S(2)}) %copy-start.1) | copy-done | bytes 8388632
  83.2 0.1 constant_dynamic-slice_fusion
  83.2 1.6 collective-permute-start
  84.8 23.9 %collective-permute-done = bf16[512,1024]{1,0:T(8,128)(2,1)} collective-permute-done((bf16[512,1024]{1,0:T(8,128)(2,1)S(1)}, bf16[512,1024]{1,0:T(8,128)(2,1)}, u32[]{:S(2)}, u32[]{:S(2)}) %collective-permute-start) | collective-permute-done | bytes 1048608 | tf_op jit(solution)/shard_map/ppermute | solution.py:13
  108.7 2.4 maximum_select_fusion.2
  111.1 0.0 copy-start.2
  111.1 2.5 collective-permute-start.1
  113.6 0.8 dynamic-slice_convert_fusion.1
  114.4 0.0 copy-done.2
  114.4 89.7 %collective-permute-done.1 = bf16[512,2048]{1,0:T(8,128)(2,1)} collective-permute-done((bf16[512,2048]{1,0:T(8,128)(2,1)S(1)}, bf16[512,2048]{1,0:T(8,128)(2,1)}, u32[]{:S(2)}, u32[]{:S(2)}) %collective-permute-start.1) | collective-permute-done | bytes 2097184 | tf_op jit(solution)/shard_map/ppermute | solution.py:13
  204.1 0.2 broadcast_in_dim.15
  204.3 12.1 %fusion.8 = (bf16[512,1024]{1,0:T(8,128)(2,1)}, f32[512,1024]{1,0:T(8,128)}) fusion(f32[64,8,8,128]{3,2,1,0:T(8,128)S(1)} %bitcast.23, bf16[4096,1024]{1,0:T(8,128)(2,1)} %copy-done.1, bf16[512,2048]{1,0:T(8,128)(2,1)} %collective-permute-done.1, bf16[512,2048]{1,0:T(8,128)(2,1)} %copy-done.2, pred[]{:T(512)S(6)} %eq.6), kind=kOutput, calls=%fused_computation.15 | convolution fusion | flops 4314890240 | bytes 17825792 | tf_op jit(solution)/shard_map/dot_general | solution.py:22
  216.4 0.0 all-gather.5.cloned.1.call-update
  216.4 80.9 %all-gather.5.cloned.1.call-done = bf16[512,4096]{1,0:T(8,128)(2,1)} async-done(((bf16[512,1024]{1,0:T(8,128)(2,1)}), bf16[512,4096]{1,0:T(8,128)(2,1)}) %all-gather.5.cloned.1.call-update) | async-done | bytes 4194320 | tf_op jit(solution)/shard_map/all_gather | solution.py:53
  297.3 10.9 %fusion.7 = bf16[512,1024]{1,0:T(8,128)(2,1)} fusion(f32[64,8,8,128]{3,2,1,0:T(8,128)S(1)} %bitcast.24, f32[512,1024]{1,0:T(8,128)} %get-tuple-element.6, bf16[512,4096]{1,0:T(8,128)(2,1)} %all-gather.5.cloned.1.call-done, bf16[4096,1024]{1,0:T(8,128)(2,1)} %copy-done.1), kind=kOutput, calls=%fused_computation.13 | convolution fusion | flops 4298113024 | bytes 17825792 | tf_op jit(solution)/shard_map/dot_general | solution.py:22
  (3 shorter events, 0.0 us)
Async XLA Ops:
  6.5 59.7 %all-gather.3.cloned.1.call-start = ((), (), s32[]{:S(2)}) async-start(), calls=%async_computation | async-start | bytes 9437184 | tf_op jit(solution)/shard_map/all_gather | solution.py:31
  7.3 290.1 %all-gather.5.cloned.1.call-start = ((), (), s32[]{:S(2)}) async-start(), calls=%async_computation.1 | async-start | bytes 5242880 | tf_op jit(solution)/shard_map/all_gather | solution.py:53
  74.6 3.4 %copy-start = (bf16[32,128,1024]{2,1,0:T(8,128)(2,1)S(1)}, bf16[32,128,1024]{2,1,0:T(8,128)(2,1)}, u32[]{:S(2)}) copy-start(bf16[32,128,1024]{2,1,0:T(8,128)(2,1)} %gather_fusion) | copy-start | bytes 25165828
  79.9 3.2 %copy-start.1 = (bf16[4096,1024]{1,0:T(8,128)(2,1)}, bf16[4096,1024]{1,0:T(8,128)(2,1)S(1)}, u32[]{:S(2)}) copy-start(bf16[4096,1024]{1,0:T(8,128)(2,1)S(1)} %bitcast_multiply_fusion) | copy-start | bytes 25165828
  83.2 25.5 %collective-permute-start = (bf16[512,1024]{1,0:T(8,128)(2,1)S(1)}, bf16[512,1024]{1,0:T(8,128)(2,1)}, u32[]{:S(2)}, u32[]{:S(2)}) collective-permute-start(bf16[512,1024]{1,0:T(8,128)(2,1)S(1)} %constant_dynamic-slice_fusion), channel_id=1, source_target_pairs={{0,1},{1,0},{2,3},{3,2},{4,5},{5,4},{6,7},{7,6},{8,9},{9,8},{10,11... | collective-permute-start | bytes 3145736 | tf_op jit(solution)/shard_map/ppermute | solution.py:13
  111.1 3.2 %copy-start.2 = (bf16[512,2048]{1,0:T(8,128)(2,1)}, bf16[512,2048]{1,0:T(8,128)(2,1)S(1)}, u32[]{:S(2)}) copy-start(bf16[512,2048]{1,0:T(8,128)(2,1)S(1)} %maximum_select_fusion.2) | copy-start | bytes 6291460
  111.1 92.9 %collective-permute-start.1 = (bf16[512,2048]{1,0:T(8,128)(2,1)S(1)}, bf16[512,2048]{1,0:T(8,128)(2,1)}, u32[]{:S(2)}, u32[]{:S(2)}) collective-permute-start(bf16[512,2048]{1,0:T(8,128)(2,1)S(1)} %maximum_select_fusion.2), channel_id=1, source_target_pairs={{0,2},{1,3},{2,0},{3,1},{4,6},{5,7},{6,4},{7,5},{8,10},{9,11},{10,... | collective-permute-start | bytes 6291464 | tf_op jit(solution)/shard_map/ppermute | solution.py:13
Sparse Core Ops, SparseCore 0:
  9.2 56.9 all-gather.2
  216.6 80.7 all-gather.4
